TPU v7x, 256 devices: a whole 4x4x8 slice. The times are simulated.
256 devices in a mesh: energy: 64 (over x, z_hi, y), space: 4 (over z_lo, core).
Axes of the slice: x: 4, y: 4, z: 8 (z_hi: 4, z_lo: 2; z = z_hi * 2 + z_lo), core: 2. Of those that a mesh axis runs over, the one named last changes fastest.
Arguments:
- g_lesser: bfloat16 [64, 2, 4, 512, 512], P('energy', None, 'space'), may hold values from -6 to 6, as said below
- w_lesser: bfloat16 [64, 2, 4, 512, 512], P('energy', None, 'space'), may hold values from -6 to 6, as said below
- g_retarded: bfloat16 [64, 2, 4, 4, 512, 512], P('energy', None, 'space'), may hold values from -0.1875 to 0.1875
- energy_index: int32 [64], replicated, may hold values from 0 to 63, each once
Outputs:
- sigma_lesser: bfloat16 [64, 2, 4, 512, 512], P('energy', None, 'space')
- delta_green: bfloat16 [64, 2, 4, 512, 512], P('energy', None, 'space')
Inputs may be any that keep to these rules, and one draw needn't show every extreme that they name: `g_lesser`: anti-Hermitian in every diagonal block at every energy: element (j, i) of component 0 is minus element (i, j), of component 1 equal to it. `w_lesser`: anti-Hermitian in every diagonal block at every energy: element (j, i) of component 0 is minus element (i, j), of component 1 equal to it. `energy_index`: each grid point once.
All inputs are finite; a program needn't handle non-finite values.
Results may differ from a plain program's by a relative error of at most 0.013.
Values may be sent and summed in bfloat16 or wider, within the bound.
A program may use at most 128 MiB of HBM per device.

v0:
```python
import math
import jax
import jax.numpy as jnp
from jax import lax
from jax.sharding import PartitionSpec as P


def twiddles(energy_index, per_device, groups):
    grid_size = energy_index.shape[0]
    padded_len = 2 * grid_size
    row_count = 2 * grid_size
    row_ids = lax.iota(jnp.int32, row_count)
    local_energy = row_ids // (2 * groups)
    component = row_ids // groups % 2
    source = row_ids % groups
    stored = source * per_device + local_energy
    grid_point = energy_index[stored]
    frequency = lax.iota(jnp.int32, padded_len)
    forward_phase = frequency[:, None] * grid_point[None, :] % padded_len
    forward_angle = forward_phase.astype(jnp.float32) * (2.0 * math.pi / padded_len)
    cos_fwd = jnp.cos(forward_angle)
    sin_fwd = jnp.sin(forward_angle)
    real_column = (component == 0)[None, :]
    forward = jnp.concatenate(
        [jnp.where(real_column, cos_fwd, sin_fwd), jnp.where(real_column, -sin_fwd, cos_fwd)],
        axis=0,
    )
    shifted = grid_point + grid_size // 2
    backward_phase = shifted[:, None] * frequency[None, :] % padded_len
    backward_angle = backward_phase.astype(jnp.float32) * (2.0 * math.pi / padded_len)
    cos_back = jnp.cos(backward_angle)
    sin_back = jnp.sin(backward_angle)
    real_row = (component == 0)[:, None]
    factor = grid_size ** (-0.5) / padded_len
    left_half = jnp.where(real_row, -sin_back, cos_back) * factor
    right_half = jnp.where(real_row, -cos_back, -sin_back) * factor
    backward = jnp.concatenate([left_half, right_half], axis=1)
    return (forward, backward)


def transform(matrix_high, matrix_low, operand):
    return jnp.dot(matrix_high, operand, preferred_element_type=jnp.float32) + jnp.dot(
        matrix_low, operand, preferred_element_type=jnp.float32
    )


def convolve(green_rows, screen_rows, forward, backward):
    padded_len = forward.shape[0] // 2
    forward_high = forward.astype(jnp.bfloat16)
    forward_low = (forward - forward_high.astype(jnp.float32)).astype(jnp.bfloat16)
    green_hat = transform(forward_high, forward_low, green_rows)
    screen_hat = transform(forward_high, forward_low, screen_rows)
    green_real = green_hat[:padded_len]
    green_imag = green_hat[padded_len:]
    screen_real = screen_hat[:padded_len]
    screen_imag = screen_hat[padded_len:]
    prod_real = green_real * screen_real - green_imag * screen_imag
    prod_imag = green_real * screen_imag + green_imag * screen_real
    merged = jnp.concatenate([prod_real, prod_imag], axis=0)
    return jnp.dot(backward, merged, precision=lax.Precision.HIGH).astype(jnp.bfloat16)


def shards(g_lesser, w_lesser, g_retarded, energy_index):
    energies_here = g_lesser.shape[0]
    width = g_lesser.shape[3]
    groups = lax.axis_size("energy")
    forward, backward = twiddles(energy_index, energies_here, groups)
    own_row = g_retarded[:, :, 0]
    columns = width * width // groups
    green = g_lesser.reshape(energies_here, 2, groups, columns)
    screen = w_lesser.reshape(energies_here, 2, groups, columns)
    green_el, screen_el = (
        lax.all_to_all(green, "energy", split_axis=2, concat_axis=2, tiled=True),
        lax.all_to_all(screen, "energy", split_axis=2, concat_axis=2, tiled=True),
    )
    sigma_el = convolve(
        green_el.reshape(-1, columns), screen_el.reshape(-1, columns), forward, backward
    )
    sigma_el = sigma_el.reshape(energies_here, 2, groups, columns)
    sigma_back = lax.all_to_all(sigma_el, "energy", split_axis=2, concat_axis=2, tiled=True)
    sigma_lesser = sigma_back.reshape(energies_here, 2, 1, width, width)
    first_prod = jnp.einsum(
        "ecnij,ednjl->encdil",
        own_row,
        lax.all_gather(sigma_lesser, "space", axis=2, tiled=True),
        preferred_element_type=jnp.float32,
    )
    left_product = jnp.stack(
        [
            first_prod[:, :, 0, 0] - first_prod[:, :, 1, 1],
            first_prod[:, :, 0, 1] + first_prod[:, :, 1, 0],
        ],
        axis=1,
    ).astype(jnp.bfloat16)
    second_prod = jnp.einsum(
        "ecnil,ednml->ecdim", left_product, own_row, preferred_element_type=jnp.float32
    )
    out_real = second_prod[:, 0, 0] + second_prod[:, 1, 1]
    out_imag = second_prod[:, 1, 0] - second_prod[:, 0, 1]
    delta = jnp.stack([out_real, out_imag], axis=1)
    delta_green = delta.astype(jnp.bfloat16).reshape(energies_here, 2, 1, width, width)
    return (sigma_lesser, delta_green)


def solution(mesh):
    return jax.shard_map(
        shards,
        mesh=mesh,
        in_specs=(
            P("energy", None, "space", None, None),
            P("energy", None, "space", None, None),
            P("energy", None, "space", None, None, None),
            P(),
        ),
        out_specs=(P("energy", None, "space", None, None), P("energy", None, "space", None, None)),
        check_vma=False,
    )
```

profile of v0, /device:TPU:1, one launch (start us, length us, event | category | flops | bytes accessed | tf_op | source)
XLA Modules:
  0.0 215.1 jit_solution(1046797866290290498)
XLA Ops:
  7.2 0.0 copy-start
  7.2 0.0 copy-start.4
  7.2 1.6 reshape.274
  8.8 2.1 copy.28
  10.9 15.1 %all-to-all-start.1 = ((bf16[1,2,64,4096]{3,1,0,2:T(2,128)(2,1)}), bf16[1,2,64,4096]{3,1,0,2:T(2,128)(2,1)S(1)}, u32[]{:S(2)}, u32[]{:S(2)}) async-start(bf16[1,2,64,4096]{3,1,0,2:T(2,128)(2,1)} %copy.28), calls=%async_computation.1 | async-start | bytes 2097152 | tf_op jit(solution)/shard_map/all_to_all | solution.py:74
  26.0 0.0 copy-done.4
  26.0 0.5 reshape.272
  26.6 2.1 copy.26
  28.6 25.1 %all-to-all-done.1 = bf16[1,2,64,4096]{3,1,0,2:T(2,128)(2,1)S(1)} async-done(((bf16[1,2,64,4096]{3,1,0,2:T(2,128)(2,1)}), bf16[1,2,64,4096]{3,1,0,2:T(2,128)(2,1)S(1)}, u32[]{:S(2)}, u32[]{:S(2)}) %all-to-all-start.1) | async-done | bytes 1048608 | tf_op jit(solution)/shard_map/all_to_all | solution.py:74
  53.7 8.3 %all-to-all-start = ((bf16[1,2,64,4096]{3,1,0,2:T(2,128)(2,1)}), bf16[1,2,64,4096]{3,1,0,2:T(2,128)(2,1)S(1)}, u32[]{:S(2)}, u32[]{:S(2)}) async-start(bf16[1,2,64,4096]{3,1,0,2:T(2,128)(2,1)} %copy.26), calls=%async_computation | async-start | bytes 2097152 | tf_op jit(solution)/shard_map/all_to_all | solution.py:73
  62.0 0.2 all-gather.2.cloned.1.call-start
  62.3 0.0 copy-done
  62.3 1.2 gather_fusion
  63.6 0.6 select_multiply_fusion.1
  64.2 0.6 copy.29
  64.8 0.7 fusion.36
  65.5 2.6 %convolution_add_fusion = f32[256,4096]{1,0:T(8,128)} fusion(f32[256,4096]{1,0:T(8,128)S(1)} %fusion.36, bf16[128,4096]{1,0:T(8,128)(2,1)S(1)} %bitcast.74, f32[128,128]{1,0:T(8,128)S(1)} %get-tuple-element.18, f32[128,128]{1,0:T(8,128)S(1)} %get-tuple-element.19), kind=kOutput, calls=%fused_computation.2 | convolution fusion | flops 269647872 | bytes 9568256 | tf_op jit(solution)/shard_map/dot_general | solution.py:42
  68.1 22.7 %all-to-all-done = bf16[1,2,64,4096]{3,1,0,2:T(2,128)(2,1)S(1)} async-done(((bf16[1,2,64,4096]{3,1,0,2:T(2,128)(2,1)}), bf16[1,2,64,4096]{3,1,0,2:T(2,128)(2,1)S(1)}, u32[]{:S(2)}, u32[]{:S(2)}) %all-to-all-start) | async-done | bytes 1048608 | tf_op jit(solution)/shard_map/all_to_all | solution.py:73
  90.8 0.6 copy.27
  91.3 0.7 fusion.38
  92.0 0.0 copy-start.2
  92.0 0.7 convolution_add_fusion.1
  92.8 1.5 copy-done.2
  94.2 0.9 multiply_subtract_fusion
  95.2 1.5 convolution_convert_fusion
  96.7 1.1 copy.30
  97.8 32.1 %all_to_all.15 = bf16[1,2,64,4096]{3,1,0,2:T(2,128)(2,1)S(1)} all-to-all(bf16[1,2,64,4096]{3,1,0,2:T(2,128)(2,1)S(1)} %copy.30), channel_id=1, replica_groups=mesh['energy'=64,'space'=4] {'energy'}, dimensions={2} | all-to-all | bytes 2097152 | tf_op jit(solution)/shard_map/all_to_all | solution.py:80
  130.0 0.6 copy.31
  130.6 1.3 reshape.277
  131.9 0.0 all-gather.2.cloned.1.call-update
  131.9 47.4 %all-gather.2.cloned.1.call-done = bf16[1,2,4,512,512]{4,3,1,0,2:T(8,128)(2,1)} async-done(((bf16[1,2,1,512,512]{4,3,1,0,2:T(8,128)(2,1)}), bf16[1,2,4,512,512]{4,3,1,0,2:T(8,128)(2,1)}) %all-gather.2.cloned.1.call-update) | async-done | bytes 4194320 | tf_op jit(solution)/shard_map/all_gather | solution.py:85
  179.3 14.1 %convolution_bitcast_fusion = f32[1,4,2,2,512,512]{4,5,2,3,1,0:T(8,128)} fusion(bf16[1,2,4,512,512]{4,3,1,0,2:T(8,128)(2,1)} %all-gather.2.cloned.1.call-done, bf16[1,2,1,4,512,512]{5,4,3,2,1,0:T(8,128)(2,1)} %param.6), kind=kOutput, calls=%fused_computation.1 | convolution fusion | flops 4294967296 | bytes 25165824 | tf_op jit(solution)/shard_map/ecnij,ednjl->encdil/dot_general | solution.py:82
  193.4 4.2 %fusion.13 = bf16[1,4,512,512]{2,3,1,0:T(8,128)(2,1)S(1)} fusion(f32[1,4,2,2,512,512]{4,5,2,3,1,0:T(8,128)} %convolution_bitcast_fusion), kind=kLoop, calls=%fused_computation.22 | loop fusion | flops 2097152 | bytes 10485760 | tf_op jit(solution)/shard_map/add | solution.py:91
  197.6 0.0 copy-start.3
  197.6 4.4 %fusion.12 = bf16[1,4,512,512]{2,3,1,0:T(8,128)(2,1)S(1)} fusion(f32[1,4,2,2,512,512]{4,5,2,3,1,0:T(8,128)} %convolution_bitcast_fusion), kind=kLoop, calls=%fused_computation.21 | loop fusion | flops 2097152 | bytes 10485760 | tf_op jit(solution)/shard_map/sub | solution.py:90
  202.1 0.2 copy-done.3
  202.3 0.0 copy-start.1
  202.3 4.5 %fusion.11 = f32[1,2,2,512,512]{4,3,2,1,0:T(8,128)S(1)} fusion(bf16[1,4,512,512]{2,3,1,0:T(8,128)(2,1)S(1)} %fusion.13, bf16[1,4,512,512]{2,3,1,0:T(8,128)(2,1)S(1)} %fusion.12, bf16[1,2,1,4,512,512]{5,4,3,2,1,0:T(8,128)(2,1)S(1)} %copy-done.3), kind=kOutput, calls=%fused_computation.20 | convolution fusion | flops 4303355904 | bytes 12582912 | tf_op jit(solution)/shard_map/ecnil,ednml->ecdim/dot_general | solution.py:95
  206.8 0.4 fusion.15
  207.2 1.1 pad_maximum_fusion
  208.2 0.0 copy-done.1
  (4 shorter events, 0.0 us)
Async XLA Ops:
  7.2 55.1 %copy-start = (s32[64]{0:T(128)S(1)}, s32[64]{0:T(128)}, u32[]{:S(2)}) copy-start(s32[64]{0:T(128)} %param.7) | copy-start | bytes 772
  7.2 18.8 %copy-start.4 = (bf16[1,2,1,512,512]{4,3,2,1,0:T(8,128)(2,1)S(1)}, bf16[1,2,1,512,512]{4,3,2,1,0:T(8,128)(2,1)}, u32[]{:S(2)}) copy-start(bf16[1,2,1,512,512]{4,3,2,1,0:T(8,128)(2,1)} %param.4) | copy-start | bytes 3145732
  10.9 42.8 %all-to-all-start.1 = ((bf16[1,2,64,4096]{3,1,0,2:T(2,128)(2,1)}), bf16[1,2,64,4096]{3,1,0,2:T(2,128)(2,1)S(1)}, u32[]{:S(2)}, u32[]{:S(2)}) async-start(bf16[1,2,64,4096]{3,1,0,2:T(2,128)(2,1)} %copy.28), calls=%async_computation.1 | async-start | bytes 2097152 | tf_op jit(solution)/shard_map/all_to_all | solution.py:74
  53.7 37.0 %all-to-all-start = ((bf16[1,2,64,4096]{3,1,0,2:T(2,128)(2,1)}), bf16[1,2,64,4096]{3,1,0,2:T(2,128)(2,1)S(1)}, u32[]{:S(2)}, u32[]{:S(2)}) async-start(bf16[1,2,64,4096]{3,1,0,2:T(2,128)(2,1)} %copy.26), calls=%async_computation | async-start | bytes 2097152 | tf_op jit(solution)/shard_map/all_to_all | solution.py:73
  62.0 117.3 %all-gather.2.cloned.1.call-start = ((), (), s32[]{:S(2)}) async-start(), calls=%async_computation.3 | async-start | bytes 5242880 | tf_op jit(solution)/shard_map/all_gather | solution.py:85
  92.0 2.2 %copy-start.2 = (f32[256,4096]{1,0:T(8,128)S(1)}, f32[256,4096]{1,0:T(8,128)}, u32[]{:S(2)}) copy-start(f32[256,4096]{1,0:T(8,128)} %convolution_add_fusion) | copy-start | bytes 12582916
  197.6 4.6 %copy-start.3 = (bf16[1,2,1,4,512,512]{5,4,3,2,1,0:T(8,128)(2,1)S(1)}, bf16[1,2,1,4,512,512]{5,4,3,2,1,0:T(8,128)(2,1)}, u32[]{:S(2)}) copy-start(bf16[1,2,1,4,512,512]{5,4,3,2,1,0:T(8,128)(2,1)} %param.6) | copy-start | bytes 12582916
  202.3 6.0 %copy-start.1 = (s32[64]{0:T(128)S(1)}, s32[64]{0:T(128)}, u32[]{:S(2)}) copy-start(s32[64]{0:T(128)} %param.7) | copy-start | bytes 772
Sparse Core Ops, SparseCore 0:
  132.0 47.2 all-gather.1
where the time goes:
time: 215 us
  waiting for transfers between devices  95.2 us (44%)
  blocking collectives  32.1 us (15%)
  matrix products  24.9 us (12%)
  starting transfers between devices  23.7 us (11%)
  between operations  14.2 us (7%)
  local copies, waits for them, and re-layouts  13.4 us (6%)
  other arithmetic  11.6 us (5%)
    all_gather x1, waiting for transfers between devices, shards(): lax.all_gather(sigma_lesser, 'space', axis=2, tiled=True)  47.4 us
    all_to_all x1, blocking collectives, shards(): lax.all_to_all(sigma_el, 'energy', split_axis=2, concat_axis=2, tiled=True)  32.1 us
    all_to_all x1, waiting for transfers between devices, shards(): lax.all_to_all(screen, 'energy', split_axis=2, concat_axis=2, tiled=True)  25.1 us
    all_to_all x1, waiting for transfers between devices, shards(): lax.all_to_all(green, 'energy', split_axis=2, concat_axis=2, tiled=True)  22.7 us
    all_to_all x1, starting transfers between devices, shards(): lax.all_to_all(screen, 'energy', split_axis=2, concat_axis=2, tiled=True)  15.1 us
    dot_general x1, matrix products, shards(): jnp.einsum('ecnij,ednjl->encdil', own_row, lax.all_gather(sigma_lesser, '...  14.1 us
    all_to_all x1, starting transfers between devices, shards(): lax.all_to_all(green, 'energy', split_axis=2, concat_axis=2, tiled=True)  8.33 us
    dot_general x1, matrix products, shards(): jnp.einsum('ecnil,ednml->ecdim', left_product, own_row, preferred_element...  4.54 us
  transfers between devices with their start and end apart: 3, of which 3 were waited for; matrix products, arithmetic and copies ran while one was open for 4% of the time, Pallas kernels for 0%

commit v1 on v0

--- a/solution.py
+++ b/solution.py
@@ -3,6 +3,10 @@
 import jax.numpy as jnp
 from jax import lax
 from jax.sharding import PartitionSpec as P
+
+
+def pair_the_edges(vec, mesh_name):
+    return jnp.concatenate(lax.all_gather(vec, mesh_name), axis=2)
 
 
 def twiddles(energy_index, per_device, groups):
@@ -82,7 +86,7 @@
     first_prod = jnp.einsum(
         "ecnij,ednjl->encdil",
         own_row,
-        lax.all_gather(sigma_lesser, "space", axis=2, tiled=True),
+        pair_the_edges(sigma_lesser, "space"),
         preferred_element_type=jnp.float32,
     )
     left_product = jnp.stack(

time: 215 us -> 211 us (0.981)
  local copies, waits for them, and re-layouts: 13.4 us -> 23.1 us
  other arithmetic: 11.6 us -> 4.62 us
  matrix products: 24.9 us -> 18.4 us
    all_gather x0 -> x1, local copies, waits for them, and re-layouts: none -> 7.33 us  [pair_the_edges(): return jnp.concatenate(lax.all_gather(vec, mesh_name), axis=2)]
    dot_general x1, matrix products: 14.1 us -> 7.61 us  [shards(): jnp.einsum('ecnij,ednjl->encdil', own_row, pair_the_edges(sigma_lesser, '...]
    sub x1, other arithmetic: 4.42 us -> 0.89 us  [shards(): first_prod[:, :, 0, 0] - first_prod[:, :, 1, 1]]
    add x1, other arithmetic: 4.19 us -> 0.75 us  [shards(): first_prod[:, :, 0, 1] + first_prod[:, :, 1, 0]]
  transfers between devices with their start and end apart: 3 -> 3, of which waited for: 3 -> 3; matrix products, arithmetic and copies ran while one was open for 4% -> 5% of each run, Pallas kernels for 0% -> 0%
where the time goes in v1:
time: 211 us; the launch traced here: 210 us
  waiting for transfers between devices  93.9 us (45%)
  blocking collectives  32.1 us (15%)
  starting transfers between devices  23.7 us (11%)
  local copies, waits for them, and re-layouts  23.1 us (11%)
  matrix products  18.4 us (9%)
  between operations  14.2 us (7%)
  other arithmetic  4.62 us (2%)
    all_gather x1, waiting for transfers between devices, pair_the_edges(): return jnp.concatenate(lax.all_gather(vec, mesh_name), axis=2)  46.1 us
    all_to_all x1, blocking collectives, shards(): lax.all_to_all(sigma_el, 'energy', split_axis=2, concat_axis=2, tiled=True)  32.1 us
    all_to_all x1, waiting for transfers between devices, shards(): lax.all_to_all(screen, 'energy', split_axis=2, concat_axis=2, tiled=True)  25.1 us
    all_to_all x1, waiting for transfers between devices, shards(): lax.all_to_all(green, 'energy', split_axis=2, concat_axis=2, tiled=True)  22.7 us
    all_to_all x1, starting transfers between devices, shards(): lax.all_to_all(screen, 'energy', split_axis=2, concat_axis=2, tiled=True)  15.1 us
    all_to_all x1, starting transfers between devices, shards(): lax.all_to_all(green, 'energy', split_axis=2, concat_axis=2, tiled=True)  8.33 us
    dot_general x1, matrix products, shards(): jnp.einsum('ecnij,ednjl->encdil', own_row, pair_the_edges(sigma_lesser, '...  7.61 us
    all_gather x1, local copies, waits for them, and re-layouts, pair_the_edges(): return jnp.concatenate(lax.all_gather(vec, mesh_name), axis=2)  7.33 us
  transfers between devices with their start and end apart: 3, of which 3 were waited for; matrix products, arithmetic and copies ran while one was open for 5% of the time, Pallas kernels for 0%

profile of v1, /device:TPU:1, one launch (start us, length us, event | category | flops | bytes accessed | tf_op | source)
XLA Modules:
  0.0 210.1 jit_solution(10122084408845452529)
XLA Ops:
  7.2 0.0 copy-start
  7.2 0.0 copy-start.4
  7.2 1.6 reshape.279
  8.8 2.1 copy.25
  10.9 15.1 %all-to-all-start.1 = ((bf16[1,2,64,4096]{3,1,0,2:T(2,128)(2,1)}), bf16[1,2,64,4096]{3,1,0,2:T(2,128)(2,1)S(1)}, u32[]{:S(2)}, u32[]{:S(2)}) async-start(bf16[1,2,64,4096]{3,1,0,2:T(2,128)(2,1)} %copy.25), calls=%async_computation.1 | async-start | bytes 2097152 | tf_op jit(solution)/shard_map/all_to_all | solution.py:78
  26.0 0.0 copy-done.4
  26.0 0.5 reshape.277
  26.6 2.1 copy.23
  28.6 25.1 %all-to-all-done.1 = bf16[1,2,64,4096]{3,1,0,2:T(2,128)(2,1)S(1)} async-done(((bf16[1,2,64,4096]{3,1,0,2:T(2,128)(2,1)}), bf16[1,2,64,4096]{3,1,0,2:T(2,128)(2,1)S(1)}, u32[]{:S(2)}, u32[]{:S(2)}) %all-to-all-start.1) | async-done | bytes 1048608 | tf_op jit(solution)/shard_map/all_to_all | solution.py:78
  53.7 8.3 %all-to-all-start = ((bf16[1,2,64,4096]{3,1,0,2:T(2,128)(2,1)}), bf16[1,2,64,4096]{3,1,0,2:T(2,128)(2,1)S(1)}, u32[]{:S(2)}, u32[]{:S(2)}) async-start(bf16[1,2,64,4096]{3,1,0,2:T(2,128)(2,1)} %copy.23), calls=%async_computation | async-start | bytes 2097152 | tf_op jit(solution)/shard_map/all_to_all | solution.py:77
  62.0 0.2 all-gather.2.cloned.1.call-start
  62.3 0.0 copy-done
  62.3 1.2 gather_fusion
  63.6 0.6 select_multiply_fusion.1
  64.2 0.6 copy.26
  64.8 0.7 fusion.36
  65.5 2.6 %convolution_add_fusion = f32[256,4096]{1,0:T(8,128)} fusion(f32[256,4096]{1,0:T(8,128)S(1)} %fusion.36, bf16[128,4096]{1,0:T(8,128)(2,1)S(1)} %bitcast.78, f32[128,128]{1,0:T(8,128)S(1)} %get-tuple-element.12, f32[128,128]{1,0:T(8,128)S(1)} %get-tuple-element.13), kind=kOutput, calls=%fused_computation.2 | convolution fusion | flops 269647872 | bytes 9568256 | tf_op jit(solution)/shard_map/dot_general | solution.py:46
  68.1 22.7 %all-to-all-done = bf16[1,2,64,4096]{3,1,0,2:T(2,128)(2,1)S(1)} async-done(((bf16[1,2,64,4096]{3,1,0,2:T(2,128)(2,1)}), bf16[1,2,64,4096]{3,1,0,2:T(2,128)(2,1)S(1)}, u32[]{:S(2)}, u32[]{:S(2)}) %all-to-all-start) | async-done | bytes 1048608 | tf_op jit(solution)/shard_map/all_to_all | solution.py:77
  90.8 0.6 copy.24
  91.3 0.7 fusion.38
  92.0 0.0 copy-start.2
  92.0 0.7 convolution_add_fusion.1
  92.8 1.5 copy-done.2
  94.2 0.9 multiply_subtract_fusion
  95.2 1.5 convolution_convert_fusion
  96.7 1.1 copy.27
  97.8 32.1 %all_to_all.15 = bf16[1,2,64,4096]{3,1,0,2:T(2,128)(2,1)S(1)} all-to-all(bf16[1,2,64,4096]{3,1,0,2:T(2,128)(2,1)S(1)} %copy.27), channel_id=1, replica_groups=mesh['energy'=64,'space'=4] {'energy'}, dimensions={2} | all-to-all | bytes 2097152 | tf_op jit(solution)/shard_map/all_to_all | solution.py:84
  130.0 0.6 copy.28
  130.6 1.3 all_gather_reshape.3
  131.9 0.0 all-gather.2.cloned.1.call-update
  131.9 1.3 reshape.282
  133.2 46.1 %all-gather.2.cloned.1.call-done = bf16[4,1,2,1,512,512]{5,4,3,2,1,0:T(8,128)(2,1)} async-done(((bf16[1,1,2,1,512,512]{5,4,3,2,1,0:T(8,128)(2,1)}), bf16[4,1,2,1,512,512]{5,4,3,2,1,0:T(8,128)(2,1)}) %all-gather.2.cloned.1.call-update) | async-done | bytes 4194320 | tf_op jit(solution)/shard_map/all_gather | solution.py:9
  179.3 7.3 %copy.31 = bf16[4,1,2,1,512,512]{4,5,2,0,3,1:T(8,128)(2,1)} copy(bf16[4,1,2,1,512,512]{5,4,3,2,1,0:T(8,128)(2,1)} %all-gather.2.cloned.1.call-done) | data formatting | bytes 8388608 | tf_op jit(solution)/shard_map/all_gather | solution.py:9
  186.7 7.6 %convolution_bitcast_fusion = f32[1,4,2,2,512,512]{4,5,2,3,1,0:T(8,128)S(1)} fusion(bf16[4,1,2,1,512,512]{4,5,2,0,3,1:T(8,128)(2,1)} %copy.31, bf16[1,2,1,4,512,512]{5,4,3,2,1,0:T(8,128)(2,1)} %param.6), kind=kOutput, calls=%fused_computation.1 | convolution fusion | flops 4294967296 | bytes 25165824 | tf_op jit(solution)/shard_map/ecnij,ednjl->encdil/dot_general | solution.py:86
  194.3 0.8 fusion.13
  195.0 0.0 copy-start.3
  195.0 0.9 fusion.12
  195.9 1.3 copy-done.3
  197.2 0.0 copy-start.1
  197.2 4.5 %fusion.11 = f32[1,2,2,512,512]{4,3,2,1,0:T(8,128)S(1)} fusion(bf16[1,4,512,512]{2,3,1,0:T(8,128)(2,1)S(1)} %fusion.13, bf16[1,4,512,512]{2,3,1,0:T(8,128)(2,1)S(1)} %fusion.12, bf16[1,2,1,4,512,512]{5,4,3,2,1,0:T(8,128)(2,1)S(1)} %copy-done.3), kind=kOutput, calls=%fused_computation.20 | convolution fusion | flops 4303355904 | bytes 12582912 | tf_op jit(solution)/shard_map/ecnil,ednml->ecdim/dot_general | solution.py:99
  201.8 0.4 fusion.15
  202.1 1.1 pad_maximum_fusion
  203.2 0.0 copy-done.1
  (4 shorter events, 0.0 us)
Async XLA Ops:
  7.2 55.1 %copy-start = (s32[64]{0:T(128)S(1)}, s32[64]{0:T(128)}, u32[]{:S(2)}) copy-start(s32[64]{0:T(128)} %param.7) | copy-start | bytes 772
  7.2 18.8 %copy-start.4 = (bf16[1,2,1,512,512]{4,3,2,1,0:T(8,128)(2,1)S(1)}, bf16[1,2,1,512,512]{4,3,2,1,0:T(8,128)(2,1)}, u32[]{:S(2)}) copy-start(bf16[1,2,1,512,512]{4,3,2,1,0:T(8,128)(2,1)} %param.4) | copy-start | bytes 3145732
  10.9 42.8 %all-to-all-start.1 = ((bf16[1,2,64,4096]{3,1,0,2:T(2,128)(2,1)}), bf16[1,2,64,4096]{3,1,0,2:T(2,128)(2,1)S(1)}, u32[]{:S(2)}, u32[]{:S(2)}) async-start(bf16[1,2,64,4096]{3,1,0,2:T(2,128)(2,1)} %copy.25), calls=%async_computation.1 | async-start | bytes 2097152 | tf_op jit(solution)/shard_map/all_to_all | solution.py:78
  53.7 37.0 %all-to-all-start = ((bf16[1,2,64,4096]{3,1,0,2:T(2,128)(2,1)}), bf16[1,2,64,4096]{3,1,0,2:T(2,128)(2,1)S(1)}, u32[]{:S(2)}, u32[]{:S(2)}) async-start(bf16[1,2,64,4096]{3,1,0,2:T(2,128)(2,1)} %copy.23), calls=%async_computation | async-start | bytes 2097152 | tf_op jit(solution)/shard_map/all_to_all | solution.py:77
  62.0 117.3 %all-gather.2.cloned.1.call-start = ((), (), s32[]{:S(2)}) async-start(), calls=%async_computation.3 | async-start | bytes 5242880 | tf_op jit(solution)/shard_map/all_gather | solution.py:9
  92.0 2.2 %copy-start.2 = (f32[256,4096]{1,0:T(8,128)S(1)}, f32[256,4096]{1,0:T(8,128)}, u32[]{:S(2)}) copy-start(f32[256,4096]{1,0:T(8,128)} %convolution_add_fusion) | copy-start | bytes 12582916
  195.0 2.2 %copy-start.3 = (bf16[1,2,1,4,512,512]{5,4,3,2,1,0:T(8,128)(2,1)S(1)}, bf16[1,2,1,4,512,512]{5,4,3,2,1,0:T(8,128)(2,1)}, u32[]{:S(2)}) copy-start(bf16[1,2,1,4,512,512]{5,4,3,2,1,0:T(8,128)(2,1)} %param.6) | copy-start | bytes 12582916
  197.2 6.0 %copy-start.1 = (s32[64]{0:T(128)S(1)}, s32[64]{0:T(128)}, u32[]{:S(2)}) copy-start(s32[64]{0:T(128)} %param.7) | copy-start | bytes 772
Sparse Core Ops, SparseCore 0:
  132.0 47.2 all-gather.1
